TPU v7x, 256 devices: a whole 4x4x8 slice. The times are simulated.
256 devices in a mesh: dp: 64 (over z, y, core), mp: 4 (over x).
Axes of the slice: x: 4, y: 4, z: 8, core: 2. Of those that a mesh axis runs over, the one named last changes fastest.
Arguments:
- attention: bfloat16 [8192, 2048], P('dp', 'mp'), may hold values from -6 to 6
- residual: bfloat16 [8192, 2048], P('dp', 'mp'), may hold values from -6 to 6
- out_weight: bfloat16 [2048, 2048], P('mp', 'dp'), may hold values from -0.125 to 0.125
- ffn_gain: float32 [2048], P('mp'), may hold values from 0.1 to 1.9
- shared_gate: bfloat16 [2048, 2816], P('dp', 'mp'), may hold values from -0.125 to 0.125
- shared_up: bfloat16 [2048, 2816], P('dp', 'mp'), may hold values from -0.125 to 0.125
- shared_down: bfloat16 [2816, 2048], P('mp', 'dp'), may hold values from -0.109375 to 0.109375
- expert_gate: bfloat16 [64, 2048, 1408], P('dp', None, 'mp'), may hold values from -0.125 to 0.125
- expert_up: bfloat16 [64, 2048, 1408], P('dp', None, 'mp'), may hold values from -0.125 to 0.125
- expert_down: bfloat16 [64, 1408, 2048], P('dp', 'mp'), may hold values from -0.15625 to 0.15625
- route_ids: int32 [8192, 6], P('dp'), may hold values from 0 to 63, all different within a row; in each aligned block of 128 rows (0 to 127, 128 to 255, ...) at most 16 rows name the same one
- route_scores: float32 [8192, 6], P('dp'), may hold values from 0.05 to 1
- placement: int32 [64], replicated, may hold values from 0 to 63, each once
- next_gain: float32 [2048], P('mp'), may hold values from 0.1 to 1.9
Outputs:
- final: bfloat16 [8192, 2048], P('dp', 'mp')
- next_normed: bfloat16 [8192, 2048], P('dp', 'mp')
Inputs may be any that keep to these rules, and one draw needn't show every extreme that they name: `route_ids`: A token's 6 experts differ. In each aligned block of 128 rows (the rows of one index of dp) no expert is named by more than 16 rows, a bound that some block reaches. `placement`: each storage index is used by exactly one expert.
All inputs are finite; a program needn't handle non-finite values.
Results may differ from a plain program's by a relative error of at most 0.0075.
Values may be sent and summed in bfloat16 or wider, within the bound.
A program may use at most 128 MiB of HBM per device.

v0:
```python
import jax
import jax.numpy as jnp
from jax import lax
from jax.sharding import PartitionSpec as P

D = 2048
EPSILON = 1e-06


def matmul(left, right):
    return jnp.dot(left, right, preferred_element_type=jnp.float32)


def local(
    attention,
    residual,
    out_weight,
    ffn_gain,
    shared_gate,
    shared_up,
    shared_down,
    expert_gate,
    expert_up,
    expert_down,
    route_ids,
    route_scores,
    placement,
    next_gain,
):
    tok_rows = attention.shape[0]
    top_count = route_ids.shape[1]
    mp_count = lax.axis_size("mp")
    mp_index = lax.axis_index("mp")
    experts = lax.axis_size("dp")
    capacity = min(tok_rows, 8 * tok_rows // experts)
    model_width = D
    partial_value = matmul(attention, lax.all_gather(out_weight, "dp", axis=1, tiled=True))
    projected = lax.psum_scatter(partial_value, "mp", scatter_dimension=1, tiled=True)
    hidden = (residual.astype(jnp.float32) + projected).astype(jnp.bfloat16)
    hidden_float = hidden.astype(jnp.float32)
    squares = lax.psum(jnp.sum(hidden_float * hidden_float, axis=1), "mp")
    normed = (hidden_float * lax.rsqrt(squares / model_width + EPSILON)[:, None] * ffn_gain).astype(
        jnp.bfloat16
    )
    whole_rows = lax.all_gather(normed, "mp", axis=1, tiled=True)
    pieces = (
        lax.all_gather(shared_gate, "dp", axis=0, tiled=True),
        lax.all_gather(shared_up, "dp", axis=0, tiled=True),
    )
    shared_gval = matmul(whole_rows, pieces[0])
    shared_uval = matmul(whole_rows, pieces[1])
    shared_act = (jax.nn.silu(shared_gval) * shared_uval).astype(jnp.bfloat16)
    shared_part = matmul(shared_act, lax.all_gather(shared_down, "dp", axis=1, tiled=True))
    flat_ids = route_ids.reshape(-1)
    expert_iota = jnp.arange(experts, dtype=jnp.int32)
    one_hot = (flat_ids[:, None] == expert_iota[None, :]).astype(jnp.int32)
    target = jnp.sum(one_hot * placement[None, :], axis=1)
    slot = jnp.sum((jnp.cumsum(one_hot, axis=0) - one_hot) * one_hot, axis=1)
    token_of = jnp.arange(flat_ids.shape[0], dtype=jnp.int32) // top_count
    flat_scores = route_scores.reshape(-1)
    gate_local = expert_gate[0]
    up_local = expert_up[0]
    down_local = expert_down[0]
    quarter = capacity // mp_count
    owned = slot // quarter == mp_index
    position = jnp.where(owned, target * quarter + slot % quarter, experts * quarter)
    outgoing = (
        jnp.zeros((experts * quarter, model_width), jnp.bfloat16)
        .at[position]
        .set(whole_rows[token_of], mode="drop")
    )
    arrived = lax.all_to_all(
        outgoing.reshape(experts, quarter, model_width),
        "dp",
        split_axis=0,
        concat_axis=0,
        tiled=True,
    )
    in_rows = arrived.reshape(experts * quarter, model_width)
    pieces = (
        lax.all_gather(gate_local, "mp", axis=1, tiled=True),
        lax.all_gather(up_local, "mp", axis=1, tiled=True),
    )
    gate_val = matmul(in_rows, pieces[0])
    up_val = matmul(in_rows, pieces[1])
    activated = (jax.nn.silu(gate_val) * up_val).astype(jnp.bfloat16)
    outputs = matmul(activated, lax.all_gather(down_local, "mp", axis=0, tiled=True)).astype(
        jnp.bfloat16
    )
    returned = lax.all_to_all(
        outputs.reshape(experts, quarter, model_width),
        "dp",
        split_axis=0,
        concat_axis=0,
        tiled=True,
    )
    returned = returned.reshape(experts * quarter, model_width)
    bounded = jnp.minimum(position, experts * quarter - 1)
    weight = jnp.where(owned, flat_scores, 0.0)
    picked = returned[bounded].astype(jnp.float32) * weight[:, None]
    routed = jnp.sum(picked.reshape(tok_rows, top_count, model_width), axis=1)
    mixture = lax.psum_scatter(routed + shared_part, "mp", scatter_dimension=1, tiled=True)
    final = (hidden_float + mixture).astype(jnp.bfloat16)
    final_float = final.astype(jnp.float32)
    final_squares = lax.psum(jnp.sum(final_float * final_float, axis=1), "mp")
    next_normed = (
        final_float * lax.rsqrt(final_squares / model_width + EPSILON)[:, None] * next_gain
    ).astype(jnp.bfloat16)
    return (final, next_normed)


def solution(mesh):
    in_specs = (
        P("dp", "mp"),
        P("dp", "mp"),
        P("mp", "dp"),
        P("mp"),
        P("dp", "mp"),
        P("dp", "mp"),
        P("mp", "dp"),
        P("dp", None, "mp"),
        P("dp", None, "mp"),
        P("dp", "mp", None),
        P("dp", None),
        P("dp", None),
        P(),
        P("mp"),
    )
    out_specs = (P("dp", "mp"), P("dp", "mp"))
    return jax.shard_map(local, mesh=mesh, in_specs=in_specs, out_specs=out_specs, check_vma=False)
```

profile of v0, /device:TPU:8, one launch (start us, length us, event | category | flops | bytes accessed | tf_op | source)
XLA Modules:
  0.0 608.2 jit_solution(1089432544255874928)
XLA Ops:
  8.0 82.0 %all-gather.11.cloned.1.call-done = bf16[512,2048]{0,1:T(8,128)(2,1)} async-done(((bf16[512,32]{0,1:T(8,128)(2,1)}), bf16[512,2048]{0,1:T(8,128)(2,1)}) %all-gather.11.cloned.1.call-update) | async-done | bytes 2097168 | tf_op jit(solution)/shard_map/all_gather | solution.py:37
  90.0 3.4 fusion.50
  97.0 1.8 reduce-window.6
  99.4 18.8 %reduce-scatter.3.cloned.1.call-done = f32[128,512]{1,0:T(8,128)} async-done(((f32[128,2048]{1,0:T(8,128)}), f32[128,512]{1,0:T(8,128)}) %reduce-scatter.3.cloned.1.call-update) | async-done | bytes 262160 | tf_op jit(solution)/shard_map/reduce_scatter | solution.py:38
  119.3 8.5 %psum.14 = f32[128]{0:T(128)S(1)} all-reduce(f32[128]{0:T(128)S(1)} %get-tuple-element.8), channel_id=1, replica_groups=mesh['dp'=64,'mp'=4] {'mp'}, use_global_device_ids=true, to_apply=%region_6.7 | all-reduce | flops 128 | bytes 1024 | tf_op jit(solution)/shard_map/psum | solution.py:41
  127.9 14.2 %all_gather.25 = bf16[128,2048]{1,0:T(8,128)(2,1)S(1)} all-gather(bf16[128,512]{1,0:T(8,128)(2,1)S(1)} %fusion.32), channel_id=1, replica_groups=mesh['dp'=64,'mp'=4] {'mp'}, dimensions={1}, use_global_device_ids=true | all-gather | bytes 655360 | tf_op jit(solution)/shard_map/all_gather | solution.py:45
  142.1 20.4 %scatter_custom_fusion = bf16[256,2048]{1,0:T(8,128)(2,1)S(1)} fusion(s32[768]{0:T(1024)S(1)} %get-tuple-element.5, bf16[128,2048]{1,0:T(8,128)(2,1)S(1)} %all_gather.25, s32[1024]{0:T(1024)S(1)} %pad_clamp_fusion.1, bf16[]{:T(256)} %constant.52.clone.1), kind=kCustom, calls=%fused_computation.10 | custom fusion | bytes 1048578 | tf_op jit(solution)/shard_map/scatter | solution.py:70
  163.8 10.6 %all-to-all-start = ((bf16[64,4,2048]{2,1,0:T(4,128)(2,1)}), bf16[64,4,2048]{2,1,0:T(4,128)(2,1)S(1)}, u32[]{:S(2)}, u32[]{:S(2)}) async-start(bf16[64,4,2048]{2,1,0:T(4,128)(2,1)} %reshape.214), calls=%async_computation.1 | async-start | bytes 2097152 | tf_op jit(solution)/shard_map/all_to_all | solution.py:72
  175.1 28.0 %all-to-all-done = bf16[64,4,2048]{2,1,0:T(4,128)(2,1)S(1)} async-done(((bf16[64,4,2048]{2,1,0:T(4,128)(2,1)}), bf16[64,4,2048]{2,1,0:T(4,128)(2,1)S(1)}, u32[]{:S(2)}, u32[]{:S(2)}) %all-to-all-start) | async-done | bytes 1048608 | tf_op jit(solution)/shard_map/all_to_all | solution.py:72
  203.4 5.6 fusion.4
  209.0 41.9 %all-gather.21.cloned.1.call-done = bf16[1,2048,1408]{1,2,0:T(8,128)(2,1)} async-done(((bf16[1,2048,352]{1,2,0:T(8,128)(2,1)}), bf16[1,2048,1408]{1,2,0:T(8,128)(2,1)}) %all-gather.21.cloned.1.call-update) | async-done | bytes 5767184 | tf_op jit(solution)/shard_map/all_gather | solution.py:82
  250.9 66.3 %all-gather.23.cloned.1.call-done = bf16[1,1408,2048]{2,1,0:T(8,128)(2,1)} async-done(((bf16[1,352,2048]{2,1,0:T(8,128)(2,1)}), bf16[1,1408,2048]{2,1,0:T(8,128)(2,1)}) %all-gather.23.cloned.1.call-update) | async-done | bytes 5767184 | tf_op jit(solution)/shard_map/all_gather | solution.py:87
  317.2 8.3 %fusion.14 = bf16[256,2048]{1,0:T(8,128)(2,1)S(1)} fusion(bf16[1,1408,2048]{2,1,0:T(8,128)(2,1)} %all-gather.23.cloned.1.call-done, bf16[256,2048]{1,0:T(8,128)(2,1)S(1)} %reshape.215, bf16[1,2048,1408]{1,2,0:T(8,128)(2,1)} %all-gather.21.cloned.1.call-done, f32[256,1408]{1,0:T(8,128)} %fusion.4), kind=kOutput, calls=%fused_computation.14 | convolution fusion | flops 2955476992 | bytes 15073280 | tf_op jit(solution)/shard_map/dot_general | solution.py:11
  326.8 10.6 %all-to-all-start.1 = ((bf16[64,4,2048]{2,1,0:T(4,128)(2,1)}), bf16[64,4,2048]{2,1,0:T(4,128)(2,1)S(1)}, u32[]{:S(2)}, u32[]{:S(2)}) async-start(bf16[64,4,2048]{2,1,0:T(4,128)(2,1)} %reshape.216), calls=%async_computation.2 | async-start | bytes 2097152 | tf_op jit(solution)/shard_map/all_to_all | solution.py:90
  338.0 63.4 %all-gather.13.cloned.1.call-done = bf16[2048,704]{1,0:T(8,128)(2,1)} async-done(((bf16[32,704]{1,0:T(8,128)(2,1)}), bf16[2048,704]{1,0:T(8,128)(2,1)}) %all-gather.13.cloned.1.call-update) | async-done | bytes 2883600 | tf_op jit(solution)/shard_map/all_gather | solution.py:47
  401.4 3.2 fusion.51
  404.8 4.3 gather_fusion
  409.2 6.6 %reshape.218 = f32[128,6,2048]{2,1,0:T(8,128)} reshape(bf16[768,2048]{1,0:T(8,128)(2,1)} %gather_fusion) | data formatting | bytes 9437184 | tf_op jit(solution)/shard_map/convert_element_type | solution.py:100
  415.7 6.6 %multiply_reduce_fusion = f32[128,2048]{1,0:T(8,128)S(1)} fusion(f32[128,6,2048]{2,1,0:T(8,128)} %reshape.218, f32[128,6]{1,0:T(8,128)S(1)} %copy.31), kind=kLoop, calls=%fused_computation.3 | loop fusion | flops 2883584 | bytes 7343104 | tf_op jit(solution)/shard_map/reduce_sum | solution.py:101
  422.3 58.0 %all-gather.15.cloned.1.call-done = bf16[2048,704]{1,0:T(8,128)(2,1)} async-done(((bf16[32,704]{1,0:T(8,128)(2,1)}), bf16[2048,704]{1,0:T(8,128)(2,1)}) %all-gather.15.cloned.1.call-update) | async-done | bytes 2883600 | tf_op jit(solution)/shard_map/all_gather | solution.py:48
  480.3 78.9 %all-gather.17.cloned.1.call-done = bf16[704,2048]{0,1:T(8,128)(2,1)} async-done(((bf16[704,32]{0,1:T(8,128)(2,1)}), bf16[704,2048]{0,1:T(8,128)(2,1)}) %all-gather.17.cloned.1.call-update) | async-done | bytes 2883600 | tf_op jit(solution)/shard_map/all_gather | solution.py:53
  559.2 7.2 %convolution_add_fusion = f32[128,2048]{1,0:T(8,128)} fusion(f32[128,2048]{1,0:T(8,128)S(1)} %multiply_reduce_fusion, bf16[704,2048]{0,1:T(8,128)(2,1)} %all-gather.17.cloned.1.call-done, bf16[128,2048]{1,0:T(8,128)(2,1)S(1)} %all_gather.25, bf16[2048,704]{1,0:T(8,128)(2,1)} %all-gather.15.cloned.1.call-done, f32[128,704]{0,1:T(8,128)S(1)} %fusion.51), kind=kOutput, calls=%fused_computation.15 | convolution fusion | flops 739000320 | bytes 8749056 | tf_op jit(solution)/shard_map/dot_general | solution.py:11
  566.5 24.9 %reduce-scatter.5.cloned.1.call-done = f32[128,512]{1,0:T(8,128)} async-done(((f32[128,2048]{1,0:T(8,128)}), f32[128,512]{1,0:T(8,128)}) %reduce-scatter.5.cloned.1.call-update) | async-done | bytes 262160 | tf_op jit(solution)/shard_map/reduce_scatter | solution.py:102
  592.4 8.5 %psum.15 = f32[128]{0:T(128)S(1)} all-reduce(f32[128]{0:T(128)S(1)} %get-tuple-element.6), channel_id=1, replica_groups=mesh['dp'=64,'mp'=4] {'mp'}, use_global_device_ids=true, to_apply=%region_11.12 | all-reduce | flops 128 | bytes 1024 | tf_op jit(solution)/shard_map/psum | solution.py:105
  (62 shorter events, 12.3 us)
Async XLA Ops:
  7.2 82.8 %copy-start = (bf16[128,512]{1,0:T(8,128)(2,1)S(1)}, bf16[128,512]{1,0:T(8,128)(2,1)}, u32[]{:S(2)}) copy-start(bf16[128,512]{1,0:T(8,128)(2,1)} %param.14) | copy-start | bytes 393220
  7.2 82.8 %all-gather.11.cloned.1.call-start = ((), (), s32[]{:S(2)}) async-start(), calls=%async_computation.4 | async-start | bytes 2129920 | tf_op jit(solution)/shard_map/all_gather | solution.py:37
  7.9 110.3 %reduce-scatter.3.cloned.1.call-start = ((), (), s32[]{:S(2)}) async-start(), calls=%async_computation.5 | async-start | bytes 1310720 | tf_op jit(solution)/shard_map/reduce_scatter | solution.py:38
  93.3 3.3 copy-start.3
  93.4 5.8 copy-start.7
  93.4 24.9 %copy-start.2 = (bf16[128,512]{1,0:T(8,128)(2,1)S(1)}, bf16[128,512]{1,0:T(8,128)(2,1)}, u32[]{:S(2)}) copy-start(bf16[128,512]{1,0:T(8,128)(2,1)} %param.15) | copy-start | bytes 393220
  93.4 34.4 %copy-start.5 = (f32[512]{0:T(512)S(1)}, f32[512]{0:T(512)}, u32[]{:S(2)}) copy-start(f32[512]{0:T(512)} %param.17) | copy-start | bytes 6148
  93.4 110.0 %all-gather.19.cloned.1.call-start = ((), (), s32[]{:S(2)}) async-start(), calls=%async_computation.10 | async-start | bytes 7208960 | tf_op jit(solution)/shard_map/all_gather | solution.py:81
  94.1 156.8 %all-gather.21.cloned.1.call-start = ((), (), s32[]{:S(2)}) async-start(), calls=%async_computation.11 | async-start | bytes 7208960 | tf_op jit(solution)/shard_map/all_gather | solution.py:82
  94.7 222.5 %all-gather.23.cloned.1.call-start = ((), (), s32[]{:S(2)}) async-start(), calls=%async_computation.12 | async-start | bytes 7208960 | tf_op jit(solution)/shard_map/all_gather | solution.py:87
  95.3 306.1 %all-gather.13.cloned.1.call-start = ((), (), s32[]{:S(2)}) async-start(), calls=%async_computation.6 | async-start | bytes 3194880 | tf_op jit(solution)/shard_map/all_gather | solution.py:47
  95.9 384.4 %all-gather.15.cloned.1.call-start = ((), (), s32[]{:S(2)}) async-start(), calls=%async_computation.7 | async-start | bytes 3194880 | tf_op jit(solution)/shard_map/all_gather | solution.py:48
  163.8 39.4 %all-to-all-start = ((bf16[64,4,2048]{2,1,0:T(4,128)(2,1)}), bf16[64,4,2048]{2,1,0:T(4,128)(2,1)S(1)}, u32[]{:S(2)}, u32[]{:S(2)}) async-start(bf16[64,4,2048]{2,1,0:T(4,128)(2,1)} %reshape.214), calls=%async_computation.1 | async-start | bytes 2097152 | tf_op jit(solution)/shard_map/all_to_all | solution.py:72
  174.3 384.9 %all-gather.17.cloned.1.call-start = ((), (), s32[]{:S(2)}) async-start(), calls=%async_computation.8 | async-start | bytes 3194880 | tf_op jit(solution)/shard_map/all_gather | solution.py:53
  325.5 12.3 %copy-start.4 = (f32[128,6]{0,1:T(8,128)S(1)}, f32[128,6]{0,1:T(8,128)}, u32[]{:S(2)}) copy-start(f32[128,6]{0,1:T(8,128)} %param.25) | copy-start | bytes 9220
  326.8 77.8 %all-to-all-start.1 = ((bf16[64,4,2048]{2,1,0:T(4,128)(2,1)}), bf16[64,4,2048]{2,1,0:T(4,128)(2,1)S(1)}, u32[]{:S(2)}, u32[]{:S(2)}) async-start(bf16[64,4,2048]{2,1,0:T(4,128)(2,1)} %reshape.216), calls=%async_computation.2 | async-start | bytes 2097152 | tf_op jit(solution)/shard_map/all_to_all | solution.py:90
  337.3 254.0 %reduce-scatter.5.cloned.1.call-start = ((), (), s32[]{:S(2)}) async-start(), calls=%async_computation.9 | async-start | bytes 1310720 | tf_op jit(solution)/shard_map/reduce_scatter | solution.py:102
  422.3 178.6 %copy-start.6 = (f32[512]{0:T(512)S(1)}, f32[512]{0:T(512)}, u32[]{:S(2)}) copy-start(f32[512]{0:T(512)} %param.27) | copy-start | bytes 6148
  592.4 9.3 %copy-start.1 = (bf16[128,512]{1,0:T(8,128)(2,1)}, bf16[128,512]{1,0:T(8,128)(2,1)S(1)}, u32[]{:S(2)}) copy-start(bf16[128,512]{1,0:T(8,128)(2,1)S(1)} %get-tuple-element.7) | copy-start | bytes 393220
Sparse Core Ops, SparseCore 0:
  10.8 79.1 all-gather.10
  93.5 24.6 reduce-scatter.2
  120.2 64.3 all-gather.18
  186.4 64.4 all-gather.20
  252.7 64.4 all-gather.22
  320.2 81.0 all-gather.12
  404.5 75.7 all-gather.14
  483.4 75.7 all-gather.16
  566.6 24.7 reduce-scatter.4
where the time goes:
time: 609 us; the launch traced here: 608 us
  waiting for transfers between devices  467 us (77%)
  local copies, waits for them, and re-layouts  35.3 us (6%)
  blocking collectives  31.2 us (5%)
  matrix products  27.6 us (5%)
  starting transfers between devices  21.7 us (4%)
  between operations  14.1 us (2%)
  other arithmetic  11.7 us (2%)
    all_gather x1, waiting for transfers between devices, local(): lax.all_gather(out_weight, 'dp', axis=1, tiled=True)  82 us
    all_gather x1, waiting for transfers between devices, local(): lax.all_gather(shared_down, 'dp', axis=1, tiled=True)  78.9 us
    all_gather x1, waiting for transfers between devices, local(): lax.all_gather(down_local, 'mp', axis=0, tiled=True)  66.3 us
    all_gather x1, waiting for transfers between devices, local(): lax.all_gather(shared_gate, 'dp', axis=0, tiled=True)  63.4 us
    all_gather x1, waiting for transfers between devices, local(): lax.all_gather(shared_up, 'dp', axis=0, tiled=True)  58 us
    all_gather x1, waiting for transfers between devices, local(): lax.all_gather(up_local, 'mp', axis=1, tiled=True)  41.9 us
    all_to_all x1, waiting for transfers between devices, local(): lax.all_to_all(outgoing.reshape(experts, quarter, model_width), 'dp', spl...  28 us
    dot_general x5, matrix products, matmul(): return jnp.dot(left, right, preferred_element_type=jnp.float32)  27.6 us
  transfers between devices with their start and end apart: 11, of which 9 were waited for; matrix products, arithmetic and copies ran while one was open for 10% of the time, Pallas kernels for 0%

commit v1 on v0

--- a/solution.py
+++ b/solution.py
@@ -34,7 +34,16 @@
     experts = lax.axis_size("dp")
     capacity = min(tok_rows, 8 * tok_rows // experts)
     model_width = D
-    partial_value = matmul(attention, lax.all_gather(out_weight, "dp", axis=1, tiled=True))
+    carry_trees = lambda t0, shard_axis: jnp.concatenate(
+        lax.all_to_all(
+            jnp.stack([t0 for _ in range(lax.axis_size(shard_axis))], axis=0),
+            shard_axis,
+            split_axis=0,
+            concat_axis=0,
+        ),
+        axis=1,
+    )
+    partial_value = matmul(attention, carry_trees(out_weight, "dp"))
     projected = lax.psum_scatter(partial_value, "mp", scatter_dimension=1, tiled=True)
     hidden = (residual.astype(jnp.float32) + projected).astype(jnp.bfloat16)
     hidden_float = hidden.astype(jnp.float32)

time: 609 us -> 586 us (0.962)
  waiting for transfers between devices: 467 us -> 381 us
  blocking collectives: 31.2 us -> 94.8 us
    all_gather x1 -> x0, waiting for transfers between devices: 82 us -> none  [local(): lax.all_gather(out_weight, 'dp', axis=1, tiled=True)]
    all_to_all x0 -> x1, blocking collectives: none -> 63.2 us  [local(): lax.all_to_all(jnp.stack([t0 for _ in range(lax.axis_size(shard_axis))],...]
  transfers between devices with their start and end apart: 11 -> 10, of which waited for: 9 -> 8; matrix products, arithmetic and copies ran while one was open for 10% -> 11% of each run, Pallas kernels for 0% -> 0%
where the time goes in v1:
time: 586 us
  waiting for transfers between devices  381 us (65%)
  blocking collectives  94.8 us (16%)
  local copies, waits for them, and re-layouts  36.4 us (6%)
  matrix products  26 us (4%)
  starting transfers between devices  21.7 us (4%)
  between operations  14.4 us (2%)
  other arithmetic  11.7 us (2%)
    all_gather x1, waiting for transfers between devices, local(): lax.all_gather(shared_down, 'dp', axis=1, tiled=True)  78.9 us
    all_gather x1, waiting for transfers between devices, local(): lax.all_gather(down_local, 'mp', axis=0, tiled=True)  66.3 us
    all_gather x1, waiting for transfers between devices, local(): lax.all_gather(shared_gate, 'dp', axis=0, tiled=True)  63.2 us
    all_to_all x1, blocking collectives, local(): lax.all_to_all(jnp.stack([t0 for _ in range(lax.axis_size(shard_axis))],...  63.2 us
    all_gather x1, waiting for transfers between devices, local(): lax.all_gather(shared_up, 'dp', axis=0, tiled=True)  57.8 us
    all_gather x1, waiting for transfers between devices, local(): lax.all_gather(up_local, 'mp', axis=1, tiled=True)  41.6 us
    all_to_all x1, waiting for transfers between devices, local(): lax.all_to_all(outgoing.reshape(experts, quarter, model_width), 'dp', spl...  28 us
    dot_general x5, matrix products, matmul(): return jnp.dot(left, right, preferred_element_type=jnp.float32)  26 us
  transfers between devices with their start and end apart: 10, of which 8 were waited for; matrix products, arithmetic and copies ran while one was open for 11% of the time, Pallas kernels for 0%

profile of v1, /device:TPU:8, one launch (start us, length us, event | category | flops | bytes accessed | tf_op | source)
XLA Modules:
  0.0 585.8 jit_solution(5083724393605672194)
XLA Ops:
  8.3 63.2 %all_to_all.15 = bf16[64,512,32]{1,2,0:T(8,128)(2,1)S(1)} all-to-all(bf16[64,512,32]{1,2,0:T(8,128)(2,1)S(1)} %stack.2), channel_id=1, replica_groups=mesh['dp'=64,'mp'=4] {'dp'}, dimensions={0} | all-to-all | bytes 4194304 | tf_op jit(solution)/shard_map/all_to_all | solution.py:38
  71.4 1.8 fusion.50
  76.9 1.8 reduce-window.6
  79.3 16.3 %reduce-scatter.3.cloned.1.call-done = f32[128,512]{1,0:T(8,128)} async-done(((f32[128,2048]{1,0:T(8,128)}), f32[128,512]{1,0:T(8,128)}) %reduce-scatter.3.cloned.1.call-update) | async-done | bytes 262160 | tf_op jit(solution)/shard_map/reduce_scatter | solution.py:47
  96.7 8.5 %psum.14 = f32[128]{0:T(128)S(1)} all-reduce(f32[128]{0:T(128)S(1)} %get-tuple-element.8), channel_id=1, replica_groups=mesh['dp'=64,'mp'=4] {'mp'}, use_global_device_ids=true, to_apply=%region_6.7 | all-reduce | flops 128 | bytes 1024 | tf_op jit(solution)/shard_map/psum | solution.py:50
  105.3 14.6 %all_gather.21 = bf16[128,2048]{1,0:T(8,128)(2,1)S(1)} all-gather(bf16[128,512]{1,0:T(8,128)(2,1)S(1)} %fusion.32), channel_id=1, replica_groups=mesh['dp'=64,'mp'=4] {'mp'}, dimensions={1}, use_global_device_ids=true | all-gather | bytes 655360 | tf_op jit(solution)/shard_map/all_gather | solution.py:54
  119.9 20.4 %scatter_custom_fusion = bf16[256,2048]{1,0:T(8,128)(2,1)S(1)} fusion(s32[768]{0:T(1024)S(1)} %get-tuple-element.5, bf16[128,2048]{1,0:T(8,128)(2,1)S(1)} %all_gather.21, s32[1024]{0:T(1024)S(1)} %pad_clamp_fusion.1, bf16[]{:T(256)} %constant.52.clone.1), kind=kCustom, calls=%fused_computation.10 | custom fusion | bytes 1048578 | tf_op jit(solution)/shard_map/scatter | solution.py:79
  141.6 10.6 %all-to-all-start.1 = ((bf16[64,4,2048]{2,1,0:T(4,128)(2,1)}), bf16[64,4,2048]{2,1,0:T(4,128)(2,1)S(1)}, u32[]{:S(2)}, u32[]{:S(2)}) async-start(bf16[64,4,2048]{2,1,0:T(4,128)(2,1)} %reshape.224), calls=%async_computation.2 | async-start | bytes 2097152 | tf_op jit(solution)/shard_map/all_to_all | solution.py:81
  152.9 28.0 %all-to-all-done.1 = bf16[64,4,2048]{2,1,0:T(4,128)(2,1)S(1)} async-done(((bf16[64,4,2048]{2,1,0:T(4,128)(2,1)}), bf16[64,4,2048]{2,1,0:T(4,128)(2,1)S(1)}, u32[]{:S(2)}, u32[]{:S(2)}) %all-to-all-start.1) | async-done | bytes 1048608 | tf_op jit(solution)/shard_map/all_to_all | solution.py:81
  181.3 5.6 fusion.4
  186.8 41.6 %all-gather.18.cloned.1.call-done = bf16[1,2048,1408]{1,2,0:T(8,128)(2,1)} async-done(((bf16[1,2048,352]{1,2,0:T(8,128)(2,1)}), bf16[1,2048,1408]{1,2,0:T(8,128)(2,1)}) %all-gather.18.cloned.1.call-update) | async-done | bytes 5767184 | tf_op jit(solution)/shard_map/all_gather | solution.py:91
  228.5 66.3 %all-gather.20.cloned.1.call-done = bf16[1,1408,2048]{2,1,0:T(8,128)(2,1)} async-done(((bf16[1,352,2048]{2,1,0:T(8,128)(2,1)}), bf16[1,1408,2048]{2,1,0:T(8,128)(2,1)}) %all-gather.20.cloned.1.call-update) | async-done | bytes 5767184 | tf_op jit(solution)/shard_map/all_gather | solution.py:96
  294.8 8.3 %fusion.14 = bf16[256,2048]{1,0:T(8,128)(2,1)S(1)} fusion(bf16[1,1408,2048]{2,1,0:T(8,128)(2,1)} %all-gather.20.cloned.1.call-done, bf16[256,2048]{1,0:T(8,128)(2,1)S(1)} %reshape.225, bf16[1,2048,1408]{1,2,0:T(8,128)(2,1)} %all-gather.18.cloned.1.call-done, f32[256,1408]{1,0:T(8,128)} %fusion.4), kind=kOutput, calls=%fused_computation.14 | convolution fusion | flops 2955476992 | bytes 15073280 | tf_op jit(solution)/shard_map/dot_general | solution.py:11
  304.3 10.6 %all-to-all-start.2 = ((bf16[64,4,2048]{2,1,0:T(4,128)(2,1)}), bf16[64,4,2048]{2,1,0:T(4,128)(2,1)S(1)}, u32[]{:S(2)}, u32[]{:S(2)}) async-start(bf16[64,4,2048]{2,1,0:T(4,128)(2,1)} %reshape.226), calls=%async_computation.3 | async-start | bytes 2097152 | tf_op jit(solution)/shard_map/all_to_all | solution.py:99
  315.5 63.2 %all-gather.10.cloned.1.call-done = bf16[2048,704]{1,0:T(8,128)(2,1)} async-done(((bf16[32,704]{1,0:T(8,128)(2,1)}), bf16[2048,704]{1,0:T(8,128)(2,1)}) %all-gather.10.cloned.1.call-update) | async-done | bytes 2883600 | tf_op jit(solution)/shard_map/all_gather | solution.py:56
  378.7 3.2 fusion.51
  382.2 4.3 gather_fusion
  386.6 6.6 %reshape.228 = f32[128,6,2048]{2,1,0:T(8,128)} reshape(bf16[768,2048]{1,0:T(8,128)(2,1)} %gather_fusion) | data formatting | bytes 9437184 | tf_op jit(solution)/shard_map/convert_element_type | solution.py:109
  393.1 6.6 %multiply_reduce_fusion = f32[128,2048]{1,0:T(8,128)S(1)} fusion(f32[128,6,2048]{2,1,0:T(8,128)} %reshape.228, f32[128,6]{1,0:T(8,128)S(1)} %copy.32), kind=kLoop, calls=%fused_computation.3 | loop fusion | flops 2883584 | bytes 7343104 | tf_op jit(solution)/shard_map/reduce_sum | solution.py:110
  399.7 57.8 %all-gather.12.cloned.1.call-done = bf16[2048,704]{1,0:T(8,128)(2,1)} async-done(((bf16[32,704]{1,0:T(8,128)(2,1)}), bf16[2048,704]{1,0:T(8,128)(2,1)}) %all-gather.12.cloned.1.call-update) | async-done | bytes 2883600 | tf_op jit(solution)/shard_map/all_gather | solution.py:57
  457.5 78.9 %all-gather.14.cloned.1.call-done = bf16[704,2048]{0,1:T(8,128)(2,1)} async-done(((bf16[704,32]{0,1:T(8,128)(2,1)}), bf16[704,2048]{0,1:T(8,128)(2,1)}) %all-gather.14.cloned.1.call-update) | async-done | bytes 2883600 | tf_op jit(solution)/shard_map/all_gather | solution.py:62
  536.5 7.2 %convolution_add_fusion = f32[128,2048]{1,0:T(8,128)} fusion(f32[128,2048]{1,0:T(8,128)S(1)} %multiply_reduce_fusion, bf16[704,2048]{0,1:T(8,128)(2,1)} %all-gather.14.cloned.1.call-done, bf16[128,2048]{1,0:T(8,128)(2,1)S(1)} %all_gather.21, bf16[2048,704]{1,0:T(8,128)(2,1)} %all-gather.12.cloned.1.call-done, f32[128,704]{0,1:T(8,128)S(1)} %fusion.51), kind=kOutput, calls=%fused_computation.15 | convolution fusion | flops 739000320 | bytes 8749056 | tf_op jit(solution)/shard_map/dot_general | solution.py:11
  543.7 24.9 %reduce-scatter.5.cloned.1.call-done = f32[128,512]{1,0:T(8,128)} async-done(((f32[128,2048]{1,0:T(8,128)}), f32[128,512]{1,0:T(8,128)}) %reduce-scatter.5.cloned.1.call-update) | async-done | bytes 262160 | tf_op jit(solution)/shard_map/reduce_scatter | solution.py:111
  569.7 8.5 %psum.15 = f32[128]{0:T(128)S(1)} all-reduce(f32[128]{0:T(128)S(1)} %get-tuple-element.6), channel_id=1, replica_groups=mesh['dp'=64,'mp'=4] {'mp'}, use_global_device_ids=true, to_apply=%region_11.12 | all-reduce | flops 128 | bytes 1024 | tf_op jit(solution)/shard_map/psum | solution.py:114
  (61 shorter events, 12.6 us)
Async XLA Ops:
  7.2 64.3 %copy-start = (bf16[128,512]{1,0:T(8,128)(2,1)S(1)}, bf16[128,512]{1,0:T(8,128)(2,1)}, u32[]{:S(2)}) copy-start(bf16[128,512]{1,0:T(8,128)(2,1)} %param.14) | copy-start | bytes 393220
  7.2 88.4 %reduce-scatter.3.cloned.1.call-start = ((), (), s32[]{:S(2)}) async-start(), calls=%async_computation.5 | async-start | bytes 1310720 | tf_op jit(solution)/shard_map/reduce_scatter | solution.py:47
  73.2 3.3 copy-start.3
  73.2 5.8 copy-start.7
  73.2 22.4 %copy-start.2 = (bf16[128,512]{1,0:T(8,128)(2,1)S(1)}, bf16[128,512]{1,0:T(8,128)(2,1)}, u32[]{:S(2)}) copy-start(bf16[128,512]{1,0:T(8,128)(2,1)} %param.15) | copy-start | bytes 393220
  73.2 32.0 %copy-start.5 = (f32[512]{0:T(512)S(1)}, f32[512]{0:T(512)}, u32[]{:S(2)}) copy-start(f32[512]{0:T(512)} %param.17) | copy-start | bytes 6148
  73.2 108.0 %all-gather.16.cloned.1.call-start = ((), (), s32[]{:S(2)}) async-start(), calls=%async_computation.10 | async-start | bytes 7208960 | tf_op jit(solution)/shard_map/all_gather | solution.py:90
  74.0 154.5 %all-gather.18.cloned.1.call-start = ((), (), s32[]{:S(2)}) async-start(), calls=%async_computation.11 | async-start | bytes 7208960 | tf_op jit(solution)/shard_map/all_gather | solution.py:91
  74.7 220.1 %all-gather.20.cloned.1.call-start = ((), (), s32[]{:S(2)}) async-start(), calls=%async_computation.12 | async-start | bytes 7208960 | tf_op jit(solution)/shard_map/all_gather | solution.py:96
  75.3 303.4 %all-gather.10.cloned.1.call-start = ((), (), s32[]{:S(2)}) async-start(), calls=%async_computation.6 | async-start | bytes 3194880 | tf_op jit(solution)/shard_map/all_gather | solution.py:56
  75.9 381.6 %all-gather.12.cloned.1.call-start = ((), (), s32[]{:S(2)}) async-start(), calls=%async_computation.7 | async-start | bytes 3194880 | tf_op jit(solution)/shard_map/all_gather | solution.py:57
  141.6 39.4 %all-to-all-start.1 = ((bf16[64,4,2048]{2,1,0:T(4,128)(2,1)}), bf16[64,4,2048]{2,1,0:T(4,128)(2,1)S(1)}, u32[]{:S(2)}, u32[]{:S(2)}) async-start(bf16[64,4,2048]{2,1,0:T(4,128)(2,1)} %reshape.224), calls=%async_computation.2 | async-start | bytes 2097152 | tf_op jit(solution)/shard_map/all_to_all | solution.py:81
  152.2 384.3 %all-gather.14.cloned.1.call-start = ((), (), s32[]{:S(2)}) async-start(), calls=%async_computation.8 | async-start | bytes 3194880 | tf_op jit(solution)/shard_map/all_gather | solution.py:62
  303.1 12.3 %copy-start.4 = (f32[128,6]{0,1:T(8,128)S(1)}, f32[128,6]{0,1:T(8,128)}, u32[]{:S(2)}) copy-start(f32[128,6]{0,1:T(8,128)} %param.25) | copy-start | bytes 9220
  304.3 77.6 %all-to-all-start.2 = ((bf16[64,4,2048]{2,1,0:T(4,128)(2,1)}), bf16[64,4,2048]{2,1,0:T(4,128)(2,1)S(1)}, u32[]{:S(2)}, u32[]{:S(2)}) async-start(bf16[64,4,2048]{2,1,0:T(4,128)(2,1)} %reshape.226), calls=%async_computation.3 | async-start | bytes 2097152 | tf_op jit(solution)/shard_map/all_to_all | solution.py:99
  314.9 253.7 %reduce-scatter.5.cloned.1.call-start = ((), (), s32[]{:S(2)}) async-start(), calls=%async_computation.9 | async-start | bytes 1310720 | tf_op jit(solution)/shard_map/reduce_scatter | solution.py:111
  399.7 178.5 %copy-start.6 = (f32[512]{0:T(512)S(1)}, f32[512]{0:T(512)}, u32[]{:S(2)}) copy-start(f32[512]{0:T(512)} %param.27) | copy-start | bytes 6148
  569.6 9.3 %copy-start.1 = (bf16[128,512]{1,0:T(8,128)(2,1)}, bf16[128,512]{1,0:T(8,128)(2,1)S(1)}, u32[]{:S(2)}) copy-start(bf16[128,512]{1,0:T(8,128)(2,1)S(1)} %get-tuple-element.7) | copy-start | bytes 393220
Sparse Core Ops, SparseCore 0:
  73.3 22.2 reduce-scatter.2
  97.6 64.4 all-gather.15
  164.1 64.3 all-gather.17
  230.3 64.4 all-gather.19
  297.8 80.9 all-gather.9
  381.7 75.7 all-gather.11
  460.7 75.7 all-gather.13
  543.8 24.7 reduce-scatter.4
